TPU v7x, 32 devices: a whole 2x2x4 slice. The times are simulated.
32 devices in a mesh: seq: 8 (over z, y), mix: 4 (over x, core).
Axes of the slice: x: 2, y: 2, z: 4, core: 2. Of those that a mesh axis runs over, the one named last changes fastest.
Arguments:
- tokens: bfloat16 [8, 2048, 512], P('mix', 'seq'), may hold values from -6 to 6
- log_forget_rate: bfloat16 [8, 2048, 16], P('mix', 'seq'), may hold values from -0.7 to 0, as said below
- w_x: bfloat16 [512, 1024], P(None, 'mix'), may hold values from -0.25 to 0.25
- w_z: bfloat16 [512, 1024], P(None, 'mix'), may hold values from -0.25 to 0.25
- w_bc: bfloat16 [512, 128], replicated, may hold values from -0.25 to 0.25
- conv_x: bfloat16 [4, 1024], P(None, 'mix'), may hold values from -3 to 3
- conv_bc: bfloat16 [4, 128], replicated, may hold values from -3 to 3
- skip: bfloat16 [16], P('mix'), may hold values from 0.5 to 2
- gain: bfloat16 [1024], P('mix'), may hold values from 0.099609375 to 1.8984375
- w_out: bfloat16 [1024, 512], P('mix'), may hold values from -0.1875 to 0.1875
Outputs:
- mixed: bfloat16 [8, 2048, 512], P('mix', 'seq')
Inputs may be any that keep to these rules, and one draw needn't show every extreme that they name: `log_forget_rate`: every entry is below zero.
All inputs are finite; a program needn't handle non-finite values.
Results may differ from a plain program's by a relative error of at most 0.012.
Values may be sent and summed in bfloat16 or wider, within the bound.
A program may use at most 128 MiB of HBM per device.

v0:
```python
import jax
import jax.numpy as jnp
from jax import lax
from jax.sharding import PartitionSpec as P

HEAD_DIM = 64
STATE = 64
CONV = 4
BLOCK = 128


def shifted(value, axis, steps):
    count = lax.axis_size(axis)
    leading, last = (max(0, -steps), min(count, count - steps))
    return lax.ppermute(value, axis, [(source, source + steps) for source in range(leading, last)])


def carried_in(value, axis, join, neutral):
    count, mine = (lax.axis_size(axis), lax.axis_index(axis))
    pieces = jax.tree.map(lambda part: lax.all_gather(part, axis), value)
    total = jax.tree.map(
        lambda part, zero: jnp.full_like(part, 0) + jnp.asarray(zero, part.dtype), value, neutral
    )

    def hop(position, total):
        longer = join(total, jax.tree.map(lambda part: part[position], pieces))
        return jax.tree.map(lambda new, old: jnp.where(position < mine, new, old), longer, total)

    return lax.fori_loop(0, count - 1, hop, total)


def conv_silu(padded_sequence, taps):
    length = padded_sequence.shape[1] - CONV + 1
    total = jnp.zeros((padded_sequence.shape[0], length, padded_sequence.shape[2]), jnp.float32)
    for k in range(CONV):
        total = total + taps[k].astype(jnp.float32)[None, None, :] * padded_sequence[
            :, k : k + length
        ].astype(jnp.float32)
    return jax.nn.silu(total).astype(jnp.bfloat16)


def chain(earlier, later):
    log_e, state_e = earlier
    log_l, state_l = later
    return (log_e + log_l, jnp.exp(log_l)[..., None] * state_e + state_l)


def mixture_pass(x_act, bmat, cmat, decay, skip_f):
    length = x_act.shape[0]
    heads = x_act.shape[1] // HEAD_DIM
    count = length // BLOCK
    xb = x_act.reshape(count, BLOCK, heads, HEAD_DIM)
    input_projection_rows = bmat.reshape(count, BLOCK, STATE)
    readout_projection_rows = cmat.reshape(count, BLOCK, STATE)
    ab = decay.reshape(count, BLOCK, heads)
    cum = jnp.cumsum(ab, axis=1)
    scale_in = jnp.sqrt(-jnp.expm1(2.0 * ab))
    mask = jnp.tril(jnp.ones((BLOCK, BLOCK), bool))[None, :, :, None]
    attention_scores = jnp.einsum(
        "xsa,xza->xsz",
        readout_projection_rows,
        input_projection_rows,
        preferred_element_type=jnp.float32,
    )
    seg = cum[:, :, None, :] - cum[:, None, :, :]
    decay_mat = jnp.where(mask, jnp.exp(jnp.where(mask, seg, -jnp.inf)), 0.0)
    weights = (decay_mat * scale_in[:, None, :, :] * attention_scores[..., None]).astype(
        jnp.bfloat16
    )
    intra = jnp.einsum("bqkh,bkhp->bqhp", weights, xb, preferred_element_type=jnp.float32)
    tail = jnp.exp(cum[:, -1:, :] - cum) * scale_in
    scaled = (xb.astype(jnp.float32) * tail[..., None]).astype(jnp.bfloat16)
    block_states = jnp.einsum(
        "bkhp,bkn->bhpn", scaled, input_projection_rows, preferred_element_type=jnp.float32
    )
    block_log = cum[:, -1, :]

    def advance(state, item):
        step_log, step_state = item
        return (jnp.exp(step_log)[:, None, None] * state + step_state, state)

    init = jnp.zeros((heads, HEAD_DIM, STATE), jnp.float32)
    final, incoming = lax.scan(advance, init, (block_log, block_states))
    inter = jnp.exp(cum)[..., None] * jnp.einsum(
        "bqn,bhpn->bqhp",
        readout_projection_rows.astype(jnp.float32),
        incoming,
        precision=lax.Precision.HIGHEST,
    )
    y_local = intra + inter + skip_f[None, None, :, None] * xb.astype(jnp.float32)
    offsets = jnp.cumsum(block_log, axis=0) - block_log
    cum_dev = cum + offsets[:, None, :]
    return (
        y_local.reshape(length, heads * HEAD_DIM),
        cum_dev.reshape(length, heads),
        jnp.sum(block_log, axis=0),
        final.reshape(heads, HEAD_DIM * STATE),
    )


def body(tokens, log_forget_rate, w_x, w_z, w_bc, conv_x, conv_bc, skip, gain, w_out):
    inputs, decay_factors = (tokens, log_forget_rate)
    w_x, w_z, conv_x, skip, gain, w_out = (
        lax.all_gather(w_x, "mix", axis=1, tiled=True),
        lax.all_gather(w_z, "mix", axis=1, tiled=True),
        lax.all_gather(conv_x, "mix", axis=1, tiled=True),
        lax.all_gather(skip, "mix", axis=0, tiled=True),
        lax.all_gather(gain, "mix", axis=0, tiled=True),
        lax.all_gather(w_out, "mix", axis=0, tiled=True),
    )
    heads = w_x.shape[1] // HEAD_DIM
    mixture_batch, length = (inputs.shape[0], inputs.shape[1])
    pre_x = jnp.einsum("mld,de->mle", inputs, w_x, preferred_element_type=jnp.float32).astype(
        jnp.bfloat16
    )
    pre_bc = jnp.einsum("mld,de->mle", inputs, w_bc, preferred_element_type=jnp.float32).astype(
        jnp.bfloat16
    )
    gate_pre = jnp.einsum("mld,de->mle", inputs, w_z, preferred_element_type=jnp.float32).astype(
        jnp.bfloat16
    )
    rim_x, rim_bc = shifted(
        (pre_x[:, length - CONV + 1 :], pre_bc[:, length - CONV + 1 :]), "seq", 1
    )
    x_act = conv_silu(jnp.concatenate([rim_x, pre_x], axis=1), conv_x)
    activated_input_readout = conv_silu(jnp.concatenate([rim_bc, pre_bc], axis=1), conv_bc)
    bmat = activated_input_readout[:, :, :STATE]
    cmat = activated_input_readout[:, :, STATE:]
    skip_f = skip.astype(jnp.float32)

    def per_mixture(item):
        return mixture_pass(item[0], item[1], item[2], item[3], skip_f)

    y_local, cum_dev, dev_log, dev_state = lax.map(
        per_mixture, (x_act, bmat, cmat, decay_factors.astype(jnp.float32))
    )
    empty = (jnp.zeros_like(dev_log), jnp.zeros_like(dev_state))
    carry_log, carry_state = carried_in((dev_log, dev_state), "seq", chain, empty)
    carried = jnp.einsum(
        "mln,mhpn->mlhp",
        cmat.astype(jnp.float32),
        carry_state.reshape(mixture_batch, heads, HEAD_DIM, STATE),
        precision=lax.Precision.HIGHEST,
    )
    y = (
        y_local.reshape(mixture_batch, length, heads, HEAD_DIM)
        + jnp.exp(cum_dev)[..., None] * carried
    )
    v = y * jax.nn.silu(
        gate_pre.astype(jnp.float32).reshape(mixture_batch, length, heads, HEAD_DIM)
    )
    gain_f = gain.astype(jnp.float32).reshape(heads, HEAD_DIM)
    normed = v * lax.rsqrt(jnp.mean(v * v, axis=-1, keepdims=True) + 1e-05) * gain_f[None, None]
    normed = normed.astype(jnp.bfloat16).reshape(mixture_batch, length, heads * HEAD_DIM)
    mixed = jnp.einsum("mle,ed->mld", normed, w_out, preferred_element_type=jnp.float32)
    return mixed.astype(jnp.bfloat16)


def solution(mesh):
    return jax.shard_map(
        body,
        mesh=mesh,
        in_specs=(
            P("mix", "seq", None),
            P("mix", "seq", None),
            P(None, "mix"),
            P(None, "mix"),
            P(),
            P(None, "mix"),
            P(),
            P("mix"),
            P("mix"),
            P("mix", None),
        ),
        out_specs=P("mix", "seq", None),
        check_vma=False,
    )
```

profile of v0, /device:TPU:0, one launch (start us, length us, event | category | flops | bytes accessed | tf_op | source)
XLA Modules:
  0.0 169.5 jit_solution(146227744412121370)
XLA Ops:
  7.6 1.2 convolution_convert_fusion.3
  8.8 4.9 %collective-permute-start.1 = (bf16[2,3,128]{2,1,0:T(4,128)(2,1)S(1)}, bf16[2,3,128]{2,1,0:T(4,128)(2,1)S(1)}, u32[]{:S(2)}, u32[]{:S(2)}) collective-permute-start(bf16[2,3,128]{2,1,0:T(4,128)(2,1)S(1)} %slice.86), channel_id=1, source_target_pairs={{0,4},{4,8},{8,12},{12,16},{16,20},{20,24},{24,28},{1,5},{5,9},{9,... | collective-permute-start | bytes 4616 | tf_op jit(solution)/shard_map/ppermute | solution.py:15
  13.8 5.3 %all_gather.30 = bf16[4,1024]{1,0:T(4,128)(2,1)S(1)} all-gather(bf16[4,256]{1,0:T(4,128)(2,1)} %param.21), channel_id=1, replica_groups=mesh['seq'=8,'mix'=4] {'mix'}, dimensions={1}, use_global_device_ids=true | all-gather | bytes 10240 | tf_op jit(solution)/shard_map/all_gather | solution.py:106
  19.1 1.2 dynamic-slice
  21.0 0.9 dynamic-update-slice
  22.7 7.1 %all-reduce = bf16[16]{0:T(256)(128)(2,1)S(1)} all-reduce(bf16[16]{0:T(256)(128)(2,1)S(1)} %dynamic-update-slice), channel_id=1, replica_groups=mesh['seq'=8,'mix'=4] {'mix'}, use_global_device_ids=true, to_apply=%add | all-reduce | flops 16 | bytes 64
  29.8 0.8 copy.52
  31.7 2.0 %convolution_convert_fusion.1 = bf16[2,256,1024]{2,1,0:T(8,128)(2,1)S(1)} fusion(bf16[2,256,512]{2,1,0:T(8,128)(2,1)S(1)} %copy-done, bf16[512,1024]{1,0:T(8,128)(2,1)} %all-gather.9.cloned.1.call-done), kind=kOutput, calls=%fused_computation.52 | convolution fusion | flops 537395200 | bytes 2621440 | tf_op jit(solution)/shard_map/mld,de->mle/dot_general | solution.py:113
  33.7 3.4 %collective-permute-start = (bf16[2,3,1024]{2,1,0:T(4,128)(2,1)S(1)}, bf16[2,3,1024]{2,1,0:T(4,128)(2,1)S(1)}, u32[]{:S(2)}, u32[]{:S(2)}) collective-permute-start(bf16[2,3,1024]{2,1,0:T(4,128)(2,1)S(1)} %slice.78), channel_id=1, source_target_pairs={{0,4},{4,8},{8,12},{12,16},{16,20},{20,24},{24,28},{1,5},{5,9},{9,... | collective-permute-start | bytes 36872 | tf_op jit(solution)/shard_map/ppermute | solution.py:15
  38.6 2.3 %multiply_convert_fusion.3 = bf16[2,256,1024]{2,1,0:T(8,128)(2,1)} fusion(bf16[2,256,1024]{2,1,0:T(8,128)(2,1)S(1)} %convolution_convert_fusion.1, bf16[2,3,1024]{2,1,0:T(4,128)(2,1)S(1)} %collective-permute-done, f32[1024]{0:T(1024)S(1)} %bitcast.120, f32[1024]{0:T(1024)S(1)} %bitcast.121, f32[1024]{0:T(1024)S(1)} %bitcast.122, f32[1024]{0:T(1024)S(1)} %bitcast.119), kind=kLoop, calls=%fused_computation.49 | loop fusion | flops 13107200 | bytes 2125824 | tf_op jit(solution)/shard_map/convert_element_type | solution.py:39
  41.0 28.6 %while.44 = (s32[]{:T(128)}, f32[2,256,1024]{1,2,0:T(8,128)}, f32[2,256,16]{2,1,0:T(8,128)}, f32[2,16]{1,0:T(2,128)S(1)}, f32[2,16,4096]{2,1,0:T(8,128)}, /*inde...) while((s32[]{:T(128)}, f32[2,256,1024]{1,2,0:T(8,128)}, ...), condition=%wide.region_6.7_spmd, body=%wide.region_0.6_spmd.sunk | while | flops 312246336 | bytes 23596536 | solution.py:134
  41.0 0.9 constant_dynamic-slice_fusion.10
  43.1 1.1 constant_dynamic-slice_fusion.8
  44.9 0.9 copy.95
  46.1 2.0 %while.46 = (s32[]{:T(128)}, f32[16,64,64]{2,1,0:T(8,128)S(1)}, f32[2,16,64,64]{3,2,1,0:T(8,128)}, f32[2,16]{1,0:T(2,128)S(1)}, f32[2,16,64,64]{3,2,1,0:T(8,128)S(1)}, /*index=5*/s32[]{:T(128)}, s32[]{:T(128)}) while((s32[]{:T(128)}, f32[16,64,64]{2,1,0:T(8,128)S(1)}, f32[2,16,64,64]{3,2,1,0:T(8,128)}, f32[2,16]{1,0:T(2,128)S(1)}, ...), condition=%wide.region_3.3_spmd.clone, body=%wide.region_2.2_spmd.clone.sunk | while | flops 262147 | bytes 1573664 | solution.py:83
  46.1 0.8 bitcast_dynamic-update-slice_fusion.5
  47.1 0.8 bitcast_dynamic-update-slice_fusion.5
  48.4 0.9 convolution_bitcast_fusion.2
  49.4 2.0 %fusion.66 = f32[2,128,16,64]{1,3,2,0:T(8,128)S(1)} fusion(f32[2,128,16,64]{1,3,2,0:T(8,128)S(1)} %convolution_bitcast_fusion.2, f32[2,16,64,64]{3,2,1,0:T(8,128)} %get-tuple-element.442, bf16[2,128,16,64]{1,3,2,0:T(8,128)(2,1)S(1)} %copy.95, f32[16]{0:T(128)S(1)} %get-tuple-element.517, f32[2,128,16]{1,2,0:T(8,128)S(1)} %copy.99, ...), kind=kOutput, calls=%fused_computation.8.clone.1 | convolution fusion | flops 202637312 | bytes 3194944 | tf_op jit(solution)/shard_map/while/body/eval_jaxpr/bqn,bhpn->bqhp/dot_general | solution.py:84
  52.2 0.8 broadcast_in_dim.96
  53.1 1.1 constant_dynamic-update-slice_fusion.4
  55.3 0.9 constant_dynamic-slice_fusion.10
  57.4 1.1 constant_dynamic-slice_fusion.8
  59.2 0.9 copy.95
  60.3 2.0 %while.46 = (s32[]{:T(128)}, f32[16,64,64]{2,1,0:T(8,128)S(1)}, f32[2,16,64,64]{3,2,1,0:T(8,128)}, f32[2,16]{1,0:T(2,128)S(1)}, f32[2,16,64,64]{3,2,1,0:T(8,128)S(1)}, /*index=5*/s32[]{:T(128)}, s32[]{:T(128)}) while((s32[]{:T(128)}, f32[16,64,64]{2,1,0:T(8,128)S(1)}, f32[2,16,64,64]{3,2,1,0:T(8,128)}, f32[2,16]{1,0:T(2,128)S(1)}, ...), condition=%wide.region_3.3_spmd.clone, body=%wide.region_2.2_spmd.clone.sunk | while | flops 262147 | bytes 1573664 | solution.py:83
  60.3 0.8 bitcast_dynamic-update-slice_fusion.5
  61.3 0.8 bitcast_dynamic-update-slice_fusion.5
  62.7 0.9 convolution_bitcast_fusion.2
  63.7 2.0 %fusion.66 = f32[2,128,16,64]{1,3,2,0:T(8,128)S(1)} fusion(f32[2,128,16,64]{1,3,2,0:T(8,128)S(1)} %convolution_bitcast_fusion.2, f32[2,16,64,64]{3,2,1,0:T(8,128)} %get-tuple-element.442, bf16[2,128,16,64]{1,3,2,0:T(8,128)(2,1)S(1)} %copy.95, f32[16]{0:T(128)S(1)} %get-tuple-element.517, f32[2,128,16]{1,2,0:T(8,128)S(1)} %copy.99, ...), kind=kOutput, calls=%fused_computation.8.clone.1 | convolution fusion | flops 202637312 | bytes 3194944 | tf_op jit(solution)/shard_map/while/body/eval_jaxpr/bqn,bhpn->bqhp/dot_general | solution.py:84
  66.5 0.8 broadcast_in_dim.96
  67.4 1.1 constant_dynamic-update-slice_fusion.4
  70.2 5.1 %all-gather.3 = bf16[4,1,256]{2,1,0:T(2,128)(2,1)S(1)} all-gather(bf16[1,1,256]{2,1,0:T(2,128)(2,1)S(1)} %reshape.198), channel_id=1, replica_groups=mesh['seq'=8,'mix'=4] {'mix'}, dimensions={0}, use_global_device_ids=true | all-gather | bytes 2560 | tf_op jit(solution)/shard_map/all_gather | solution.py:108
  75.4 1.9 %fusion.24 = f32[2,256,1024]{2,1,0:T(8,128)S(1)} fusion(bf16[2,256,512]{2,1,0:T(8,128)(2,1)S(1)} %copy-done, bf16[512,1024]{1,0:T(8,128)(2,1)} %all-gather.11.cloned.1.call-done), kind=kOutput, calls=%fused_computation.51 | convolution fusion | flops 537919488 | bytes 3670016 | tf_op jit(solution)/shard_map/mld,de->mle/dot_general | solution.py:119
  77.4 1.9 %copy.58 = f32[2,256,1024]{1,2,0:T(8,128)} copy(f32[2,256,1024]{2,1,0:T(8,128)S(1)} %fusion.24) | data formatting | bytes 4194304 | tf_op jit(solution)/shard_map/reshape | solution.py:150
  79.2 20.7 %all-gather.2 = f32[8,2,16]{2,1,0:T(2,128)S(1)} all-gather(f32[1,2,16]{2,1,0:T(2,128)S(1)} %bitcast.123), channel_id=2, replica_groups=mesh['seq'=8,'mix'=4] {'seq'}, dimensions={0}, use_global_device_ids=true | all-gather | bytes 1152 | tf_op jit(solution)/shard_map/all_gather | solution.py:20
  100.1 43.5 %all-gather.15.cloned.1.call-done = f32[16,16,4096]{2,1,0:T(8,128)} async-done(((f32[2,16,4096]{2,1,0:T(8,128)}), f32[16,16,4096]{2,1,0:T(8,128)}) %all-gather.15.cloned.1.call-update) | async-done | bytes 4194320 | tf_op jit(solution)/shard_map/all_gather | solution.py:20
  143.6 8.6 %while.45 = (s32[]{:T(128)}, f32[2,16,4096]{2,1,0:T(8,128)S(1)}, s32[]{:T(128)}, f32[8,2,16]{2,1,0:T(2,128)S(1)}, f32[8,2,16,4096]{3,2,1,0:T(8,128)}, /*index=5*/s32[]{:T(128)}, s32[]{:T(128)}) while((s32[]{:T(128)}, f32[2,16,4096]{2,1,0:T(8,128)S(1)}, s32[]{:T(128)}, f32[8,2,16]{2,1,0:T(2,128)S(1)}, f32[8,2,16,4096]{3,2,1,0:T(8,128)}, ...), condition=%wide.region_8.9_spmd.clone, body=%wide.region_7.8_spmd.clone.sunk | while | flops 524292 | bytes 1573353 | solution.py:29
  143.6 1.3 fusion.67
  144.9 1.2 fusion.67
  146.1 1.2 fusion.67
  147.4 1.2 fusion.67
  148.6 1.2 fusion.67
  149.8 1.2 fusion.67
  151.0 1.2 fusion.67
  152.2 1.4 reshape.176
  153.6 3.6 %multiply_reduce_fusion = (f32[2,256,16]{1,2,0:T(8,128)S(1)}, f32[2,256,16,64]{1,3,2,0:T(8,128)S(1)}) fusion(f32[2,256,16,64]{1,3,2,0:T(8,128)S(1)} %bitcast.112, f32[2,256,16,64]{1,3,2,0:T(8,128)} %bitcast.124, f32[2,16,64,64]{3,2,1,0:T(8,128)} %reshape.176, bf16[2,256,128]{2,1,0:T(8,128)(2,1)S(1)} %copy-done.3, f32[2,256,16]{1,2,0:T(8,128)S(1)} %copy.56), kind=kOutput, calls=%fused_computation.47 | convolution fusion | flops 407363584 | bytes 7012352 | tf_op jit(solution)/shard_map/mln,mhpn->mlhp/dot_general | solution.py:139
  157.7 2.5 %all-gather.13.cloned.1.call-done = bf16[1024,512]{1,0:T(8,128)(2,1)} async-done(((bf16[256,512]{1,0:T(8,128)(2,1)}), bf16[1024,512]{1,0:T(8,128)(2,1)}) %all-gather.13.cloned.1.call-update) | async-done | bytes 1048592 | tf_op jit(solution)/shard_map/all_gather | solution.py:109
  160.2 2.8 %convolution_convert_fusion.2 = bf16[2,256,512]{2,1,0:T(8,128)(2,1)} fusion(bf16[2,256,1024]{1,2,0:T(8,128)(2,1)S(1)} %bitcast.114, bf16[1024,512]{1,0:T(8,128)(2,1)} %all-gather.13.cloned.1.call-done), kind=kOutput, calls=%fused_computation.55 | convolution fusion | flops 537133056 | bytes 2621440 | tf_op jit(solution)/shard_map/mle,ed->mld/dot_general | solution.py:155
  (122 shorter events, 15.3 us)
Async XLA Ops:
  6.5 1.0 copy-start
  6.5 25.1 %all-gather.9.cloned.1.call-start = ((), (), s32[]{:S(2)}) async-start(), calls=%async_computation | async-start | bytes 1310720 | tf_op jit(solution)/shard_map/all_gather | solution.py:104
  7.3 68.2 %all-gather.11.cloned.1.call-start = ((), (), s32[]{:S(2)}) async-start(), calls=%async_computation.1 | async-start | bytes 1310720 | tf_op jit(solution)/shard_map/all_gather | solution.py:105
  8.8 22.6 %collective-permute-start.1 = (bf16[2,3,128]{2,1,0:T(4,128)(2,1)S(1)}, bf16[2,3,128]{2,1,0:T(4,128)(2,1)S(1)}, u32[]{:S(2)}, u32[]{:S(2)}) collective-permute-start(bf16[2,3,128]{2,1,0:T(4,128)(2,1)S(1)} %slice.86), channel_id=1, source_target_pairs={{0,4},{4,8},{8,12},{12,16},{16,20},{20,24},{24,28},{1,5},{5,9},{9,... | collective-permute-start | bytes 4616 | tf_op jit(solution)/shard_map/ppermute | solution.py:15
  13.7 129.8 %all-gather.15.cloned.1.call-start = ((), (), s32[]{:S(2)}) async-start(), calls=%async_computation.3 | async-start | bytes 4718592 | tf_op jit(solution)/shard_map/all_gather | solution.py:20
  31.6 9.3 %copy-start.2 = (bf16[2,256,128]{2,1,0:T(8,128)(2,1)}, bf16[2,256,128]{2,1,0:T(8,128)(2,1)S(1)}, u32[]{:S(2)}) copy-start(bf16[2,256,128]{2,1,0:T(8,128)(2,1)S(1)} %multiply_convert_fusion.4) | copy-start | bytes 393220
  33.7 5.0 %collective-permute-start = (bf16[2,3,1024]{2,1,0:T(4,128)(2,1)S(1)}, bf16[2,3,1024]{2,1,0:T(4,128)(2,1)S(1)}, u32[]{:S(2)}, u32[]{:S(2)}) collective-permute-start(bf16[2,3,1024]{2,1,0:T(4,128)(2,1)S(1)} %slice.78), channel_id=1, source_target_pairs={{0,4},{4,8},{8,12},{12,16},{16,20},{20,24},{24,28},{1,5},{5,9},{9,... | collective-permute-start | bytes 36872 | tf_op jit(solution)/shard_map/ppermute | solution.py:15
  41.0 29.3 %copy-start.9 = (bf16[256]{0:T(256)(128)(2,1)S(1)}, bf16[256]{0:T(256)(128)(2,1)}, u32[]{:S(2)}) copy-start(bf16[256]{0:T(256)(128)(2,1)} %param.24) | copy-start | bytes 1540
  53.1 1.3 copy-start.4
  53.1 1.4 copy-start.6
  54.4 0.8 copy-start.5
  54.5 0.8 copy-start.7
  67.4 1.3 copy-start.4
  67.4 1.4 copy-start.6
  68.7 0.8 copy-start.5
  68.8 0.8 copy-start.7
  69.6 90.6 %all-gather.13.cloned.1.call-start = ((), (), s32[]{:S(2)}) async-start(), calls=%async_computation.2 | async-start | bytes 1310720 | tf_op jit(solution)/shard_map/all_gather | solution.py:109
  77.4 22.6 %copy-start.8 = (f32[2,256,16]{2,1,0:T(8,128)S(1)}, f32[2,256,16]{2,1,0:T(8,128)}, u32[]{:S(2)}) copy-start(f32[2,256,16]{2,1,0:T(8,128)} %get-tuple-element.183) | copy-start | bytes 98308
  143.6 10.0 %copy-start.1 = (f32[2,256,1024]{1,2,0:T(8,128)S(1)}, f32[2,256,1024]{1,2,0:T(8,128)}, u32[]{:S(2)}) copy-start(f32[2,256,1024]{1,2,0:T(8,128)} %copy.58) | copy-start | bytes 6291460
  143.6 10.0 %copy-start.3 = (bf16[2,256,128]{2,1,0:T(8,128)(2,1)S(1)}, bf16[2,256,128]{2,1,0:T(8,128)(2,1)}, u32[]{:S(2)}) copy-start(bf16[2,256,128]{2,1,0:T(8,128)(2,1)} %copy-done.2) | copy-start | bytes 393220
Sparse Core Ops, SparseCore 0:
  8.9 19.5 all-gather.8
  30.0 16.9 all-gather.10
  69.7 73.7 all-gather.14
  145.0 15.2 all-gather.12
where the time goes:
time: 171 us; the launch traced here: 170 us
  waiting for transfers between devices  47.3 us (28%)
  blocking collectives  38.2 us (22%)
  local copies, waits for them, and re-layouts  25.3 us (15%)
  matrix products  18.3 us (11%)
  other arithmetic  17.5 us (10%)
  between operations  14 us (8%)
  starting transfers between devices  8.44 us (5%)
    all_gather x1, waiting for transfers between devices, carried_in(): pieces = jax.tree.map(lambda part: lax.all_gather(part, axis), value)  43.5 us
    all_gather x1, blocking collectives, carried_in(): pieces = jax.tree.map(lambda part: lax.all_gather(part, axis), value)  20.7 us
    select_n x7, other arithmetic, hop(): jnp.where(position < mine, new, old)  8.38 us
    ppermute x2, starting transfers between devices, shifted(): lax.ppermute(value, axis, [(source, source + steps) for source in range(l...  8.32 us
    unnamed x1, blocking collectives  7.08 us
    dynamic_slice x6, local copies, waits for them, and re-layouts, body(): lax.map(per_mixture, (x_act, bmat, cmat, decay_factors.astype(jnp.float32)))  5.6 us
    all_gather x1, blocking collectives, body(): lax.all_gather(conv_x, 'mix', axis=1, tiled=True)  5.33 us
    all_gather x1, blocking collectives, body(): lax.all_gather(gain, 'mix', axis=0, tiled=True)  5.07 us
  transfers between devices with their start and end apart: 6, of which 2 were waited for; matrix products, arithmetic and copies ran while one was open for 33% of the time, Pallas kernels for 0%

commit v1 on v0

v1 whole, which is shorter than its diff:
```python
import functools

import jax
import jax.numpy as jnp
from jax import lax
from jax.experimental import pallas as pl
from jax.experimental.pallas import tpu as pltpu
from jax.sharding import PartitionSpec as P

HEAD_DIM = 64
STATE = 64
CONV = 4
BLOCK = 128
LANES = 128
RIM = 16
MESH = pl.DeviceIdType.MESH
F32 = jnp.float32
BF16 = jnp.bfloat16


def flipped(index, bit):
    return index + bit - 2 * bit * ((index // bit) % 2)


def dot(a, b):
    return lax.dot_general(a, b, (((1,), (0,)), ((), ())), preferred_element_type=F32)


def dot_nt(a, b):
    return lax.dot_general(a, b, (((1,), (1,)), ((), ())), preferred_element_type=F32)


def split_dot(a, b):
    high = a.astype(BF16)
    low = (a - high.astype(F32)).astype(BF16)
    return dot(high, b) + dot(low, b)


def silu(x):
    return x / (1.0 + jnp.exp(-x))


def iota(shape, dim):
    return lax.broadcasted_iota(jnp.int32, shape, dim)


def one_minus_exp(x):
    total = jnp.ones_like(x)
    for k in range(14, 1, -1):
        total = 1.0 + x * (1.0 / k) * total
    return -x * total


def kernel(
    seq, mix,
    tok, rate, wx, wz, wbc, par, cbc, wo, out,
    halo, wxb, wzb, wob, parb, logs, logsrc, pre, xact, bcs, bts, cums, tails, ecs, rows_t,
    cbm, first, yloc, sgate, normed, sbuf, rbuf, cbuf, gbuf,
    bsend, brecv, fsend, hsend, hrecv, lsend, lrecv, asend, arecv, csend, crecv,
):
    me_s, me_m = lax.axis_index("seq"), lax.axis_index("mix")
    mixtures, length = tok.shape[0], tok.shape[1]
    width = wx.shape[1]
    per = width // HEAD_DIM
    heads = rate.shape[2]
    blocks = length // BLOCK
    nrows = STATE // seq
    bits = [1 << i for i in range(mix.bit_length() - 1)]

    barrier = pltpu.get_barrier_semaphore()
    for bit in bits:
        pl.semaphore_signal(barrier, inc=1, device_id={"mix": flipped(me_m, bit)}, device_id_type=MESH)

    @pl.loop(1, seq)
    def _(i):
        pl.semaphore_signal(barrier, inc=1, device_id={"seq": (me_s + i) % seq}, device_id_type=MESH)

    pl.semaphore_wait(barrier, len(bits) + seq - 1)

    shards = ((wx, wxb), (par, parb), (wz, wzb), (wo, wob))

    def held(which, offset):
        own, slots = shards[which]
        return own if offset == 0 else slots.at[offset - 1]

    def share(which, offset, bit):
        slot = shards[which][1].at[offset + bit - 1]
        return pltpu.make_async_remote_copy(
            src_ref=held(which, offset), dst_ref=slot,
            send_sem=bsend.at[which, offset + bit - 1], recv_sem=brecv.at[which, offset + bit - 1],
            device_id={"mix": flipped(me_m, bit)}, device_id_type=MESH,
        )

    def low_bit(offset):
        return offset & -offset

    def arrived(which, offset):
        share(which, offset - low_bit(offset), low_bit(offset)).wait_recv()
        for bit in bits:
            if bit < low_bit(offset):
                share(which, offset, bit).start()

    rim_copy = pltpu.make_async_remote_copy(
        src_ref=tok.at[:, pl.ds(length - RIM, RIM), :], dst_ref=halo,
        send_sem=hsend, recv_sem=hrecv,
        device_id={"seq": (me_s + 1) % seq}, device_id_type=MESH,
    )
    rim_copy.start()
    for which in (1, 0, 2, 3):
        for bit in reversed(bits):
            share(which, 0, bit).start()

    here = iota((heads, LANES), 0)
    there = iota((heads, LANES), 1)
    order = jnp.zeros((heads, LANES), jnp.bool_)
    for offset in range(mix):
        actual = me_m
        for bit in bits:
            if offset & bit:
                actual = flipped(actual, bit)
        order = order | ((there // per == offset) & (here == actual * per + there % per))
    order = order.astype(F32).astype(BF16)
    lower = (iota((BLOCK, BLOCK), 0) >= iota((BLOCK, BLOCK), 1)).astype(F32)
    lower_b = lower.astype(BF16)

    totals = []
    for m in range(mixtures):
        device_total = jnp.zeros((1, LANES), F32)
        for b in range(blocks):
            at = pl.ds(b * BLOCK, BLOCK)
            mine = dot(rate[m, at, :], order)
            cum = dot(lower_b, mine.astype(BF16))
            gain_in = jnp.sqrt(one_minus_exp(2.0 * mine))
            last = cum[BLOCK - 1 : BLOCK]
            cums[m, at, :] = cum
            ecs[m, at, :] = jnp.exp(cum)
            tails[m, at, :] = jnp.exp(last - cum) * gain_in
            rows_t[m * blocks + b] = jnp.transpose(cum - jnp.log(gain_in))
            device_total = device_total + last
            totals.append(last)
        logsrc[pl.ds(m, 1), :] = device_total
    logsrc[pl.ds(mixtures, 8 - mixtures), :] = jnp.zeros((8 - mixtures, LANES), F32)
    logs[me_s] = logsrc[...]

    def log_copy(peer):
        return pltpu.make_async_remote_copy(
            src_ref=logsrc, dst_ref=logs.at[me_s], send_sem=lsend, recv_sem=lrecv,
            device_id={"seq": peer}, device_id_type=MESH,
        )

    @pl.loop(1, seq)
    def _(i):
        log_copy((me_s + i) % seq).start()

    inside = jnp.where(me_s > 0, 1.0, 0.0)

    def convolve(weight, taps, m, columns):
        total = jnp.zeros((length, columns), F32)
        for k in range(CONV):
            total = total + taps[k : k + 1].astype(F32) * pre[
                m, pl.ds(8 - CONV + 1 + k, length), pl.ds(0, columns)
            ]
        return silu(total)

    def project(weight, m, columns):
        edge = dot(halo[m], weight).astype(BF16).astype(F32)
        pre[m, pl.ds(0, 8), pl.ds(0, columns)] = edge[RIM - 8 :] * inside
        pre[m, pl.ds(8, length), pl.ds(0, columns)] = dot(tok[m], weight).astype(BF16).astype(F32)

    rim_copy.wait_recv()
    for m in range(mixtures):
        project(wbc[...], m, 2 * STATE)
        bc = convolve(None, cbc[...], m, 2 * STATE)
        bcs[m] = bc.astype(BF16)
        for b in range(blocks):
            part = bc[b * BLOCK : (b + 1) * BLOCK].astype(BF16)
            bts[m * blocks + b] = jnp.transpose(part.astype(F32))[:STATE].astype(BF16)
            scores = dot_nt(part[:, STATE:], part[:, :STATE])
            cbm[m * blocks + b] = scores * lower

    def spread(offset):
        return (iota((LANES, width), 0) == offset * per + iota((LANES, width), 1) // HEAD_DIM).astype(F32).astype(BF16)

    def states(offset):
        weight, params, expand = held(0, offset)[...], held(1, offset)[...], spread(offset)
        lanes = pl.ds(offset * width, width)
        per_mixture = []
        for m in range(mixtures):
            project(weight, m, width)
            x_act = convolve(None, params, m, width).astype(BF16)
            xact[m, :, lanes] = x_act
            scaled = (x_act.astype(F32) * split_dot(tails[m], expand)).astype(BF16)
            state = None
            for b in range(blocks):
                new = dot(bts[m * blocks + b], scaled[b * BLOCK : (b + 1) * BLOCK])
                if b == 0:
                    state = new
                else:
                    first[m * blocks + b - 1, :, lanes] = state
                    fade = split_dot(jnp.broadcast_to(jnp.exp(totals[m * blocks + b]), (8, LANES)), expand)[:1]
                    state = fade * state + new
            per_mixture.append(state)
        for k in range(seq):
            piece = jnp.concatenate([s[k * nrows : (k + 1) * nrows] for s in per_mixture], axis=0)
            sbuf[offset, k] = piece.astype(BF16)
        rbuf[offset, me_s] = sbuf[offset, me_s]

        @pl.loop(1, seq)
        def _(i):
            state_copy(offset, (me_s + i) % seq).start()

    def state_copy(offset, peer):
        return pltpu.make_async_remote_copy(
            src_ref=sbuf.at[offset, peer], dst_ref=rbuf.at[offset, me_s],
            send_sem=asend.at[offset], recv_sem=arecv.at[offset],
            device_id={"seq": peer}, device_id_type=MESH,
        )

    def carry_copy(offset, peer):
        return pltpu.make_async_remote_copy(
            src_ref=cbuf.at[offset, peer], dst_ref=gbuf.at[offset, me_s],
            send_sem=csend.at[offset], recv_sem=crecv.at[offset],
            device_id={"seq": peer}, device_id_type=MESH,
        )

    def wait_all(ref, sem):
        some = ref.at[pl.ds(0, seq - 1)]
        pltpu.make_async_copy(some, some, sem).wait()

    def carries(offset):
        wait_all(rbuf.at[offset], arecv.at[offset])
        expand = spread(offset)
        fade = split_dot(jnp.exp(logs[...].reshape(seq * 8, LANES)), expand)
        carry = jnp.zeros((mixtures * nrows, width), F32)
        for p in range(seq):
            cbuf[offset, p] = carry.astype(BF16)
            if p < seq - 1:
                down = jnp.concatenate(
                    [jnp.broadcast_to(fade[p * 8 + m : p * 8 + m + 1], (nrows, width)) for m in range(mixtures)], axis=0
                )
                carry = down * carry + rbuf[offset, p].astype(F32)
        gbuf[offset, me_s] = cbuf[offset, me_s]

        @pl.loop(1, seq)
        def _(i):
            carry_copy(offset, (me_s + i) % seq).start()

    group_of = iota((BLOCK, width), 1) // HEAD_DIM

    def intra(offset):
        lanes = pl.ds(offset * width, width)
        skip_row = held(1, offset)[pl.ds(CONV + 1, 1), :].astype(F32)
        for m in range(mixtures):
            for b in range(blocks):
                at = pl.ds(b * BLOCK, BLOCK)
                scores = cbm[m * blocks + b]
                cum = cums[m, at, :]
                parts = []
                for i in range(per):
                    j = offset * per + i
                    gap = cum[:, j : j + 1] - rows_t[m * blocks + b, pl.ds(j, 1), :]
                    parts.append((jnp.exp(jnp.minimum(gap, 0.0)) * scores).astype(BF16))
                x_act = xact[m, at, lanes]
                full = dot(jnp.concatenate(parts, axis=0), x_act)
                total = full[:BLOCK]
                for i in range(1, per):
                    total = jnp.where(group_of == i, full[i * BLOCK : (i + 1) * BLOCK], total)
                yloc[m, at, lanes] = total + skip_row * x_act.astype(F32)

    def gate(offset):
        lanes = pl.ds(offset * width, width)
        weight = held(2, offset)[...]
        for m in range(mixtures):
            sgate[m, :, lanes] = silu(dot(tok[m], weight).astype(BF16).astype(F32))

    same_head = (iota((width, width), 0) // HEAD_DIM == iota((width, width), 1) // HEAD_DIM).astype(F32).astype(BF16)

    def finish(offset):
        lanes = pl.ds(offset * width, width)
        wait_all(gbuf.at[offset], crecv.at[offset])
        expand = spread(offset)
        gain_row = held(1, offset)[pl.ds(CONV, 1), :].astype(F32)
        for m in range(mixtures):
            state = jnp.concatenate(
                [gbuf[offset, k].astype(F32)[m * nrows : (m + 1) * nrows] for k in range(seq)], axis=0
            )
            grow = split_dot(ecs[m], expand)
            for b in range(blocks):
                at = pl.ds(b * BLOCK, BLOCK)
                if b > 0:
                    fade = split_dot(jnp.broadcast_to(jnp.exp(totals_sum(m, b)), (8, LANES)), expand)[:1]
                    incoming = fade * state + first[m * blocks + b - 1, :, lanes]
                else:
                    incoming = state
                inter = dot(bcs[m, at, :][:, STATE:], incoming.astype(BF16))
                y = yloc[m, at, lanes] + grow[b * BLOCK : (b + 1) * BLOCK] * inter
                v = y * sgate[m, at, lanes]
                power = split_dot(v * v, same_head) * (1.0 / HEAD_DIM)
                normed[m, at, lanes] = (v * lax.rsqrt(power + 1e-05) * gain_row).astype(BF16)

    def totals_sum(m, b):
        total = totals[m * blocks]
        for k in range(1, b):
            total = total + totals[m * blocks + k]
        return total

    def take(which, offset):
        if offset:
            arrived(which, offset)

    for offset in range(mix):
        take(1, offset)
        take(0, offset)
        states(offset)
        if offset == 0:
            intra(offset)
    pltpu.make_async_copy(logs.at[pl.ds(0, seq - 1)], logs.at[pl.ds(0, seq - 1)], lrecv).wait()
    for offset in range(mix):
        carries(offset)
        take(2, offset)
        gate(offset)
    for offset in range(1, mix):
        intra(offset)
        take(3, offset)
    for offset in range(mix):
        finish(offset)
    for m in range(mixtures):
        total = jnp.zeros((length, wo.shape[1]), F32)
        for offset in range(mix):
            total = total + dot(normed[m, :, pl.ds(offset * width, width)], held(3, offset)[...])
        out[m] = total.astype(BF16)

    rim_copy.wait_send()
    for which in range(4):
        for offset in range(mix):
            for bit in bits:
                if offset == 0 or bit < low_bit(offset):
                    share(which, offset, bit).wait_send()
    wait_all(logs, lsend)
    for offset in range(mix):
        wait_all(sbuf.at[offset], asend.at[offset])
        wait_all(cbuf.at[offset], csend.at[offset])


def solution(mesh):
    seq, mix = mesh.shape["seq"], mesh.shape["mix"]

    def body(tokens, log_forget_rate, w_x, w_z, w_bc, conv_x, conv_bc, skip, gain, w_out):
        mixtures, length, depth = tokens.shape
        width = w_x.shape[1]
        inner = width * mix
        blocks = length // BLOCK
        params = jnp.concatenate(
            [
                conv_x,
                gain[None],
                jnp.repeat(skip, HEAD_DIM)[None],
                jnp.zeros((16 - CONV - 2, width), BF16),
            ],
            axis=0,
        )
        vmem = pl.BlockSpec(memory_space=pltpu.VMEM)
        dma = pltpu.SemaphoreType.DMA
        rows = mixtures * (STATE // seq)
        return pl.pallas_call(
            functools.partial(kernel, seq, mix),
            out_shape=jax.ShapeDtypeStruct((mixtures, length, w_out.shape[1]), BF16),
            in_specs=[vmem] * 8,
            out_specs=vmem,
            scratch_shapes=[
                pltpu.VMEM((mixtures, RIM, depth), BF16),
                pltpu.VMEM((mix - 1,) + w_x.shape, BF16),
                pltpu.VMEM((mix - 1,) + w_z.shape, BF16),
                pltpu.VMEM((mix - 1,) + w_out.shape, BF16),
                pltpu.VMEM((mix - 1, 16, width), BF16),
                pltpu.VMEM((seq, 8, LANES), F32),
                pltpu.VMEM((8, LANES), F32),
                pltpu.VMEM((mixtures, 8 + length, width), F32),
                pltpu.VMEM((mixtures, length, inner), BF16),
                pltpu.VMEM((mixtures, length, 2 * STATE), BF16),
                pltpu.VMEM((mixtures * blocks, STATE, BLOCK), BF16),
                pltpu.VMEM((mixtures, length, LANES), F32),
                pltpu.VMEM((mixtures, length, LANES), F32),
                pltpu.VMEM((mixtures, length, LANES), F32),
                pltpu.VMEM((mixtures * blocks, LANES, BLOCK), F32),
                pltpu.VMEM((mixtures * blocks, BLOCK, BLOCK), F32),
                pltpu.VMEM((mixtures * blocks, STATE, inner), F32),
                pltpu.VMEM((mixtures, length, inner), F32),
                pltpu.VMEM((mixtures, length, inner), F32),
                pltpu.VMEM((mixtures, length, inner), BF16),
                pltpu.VMEM((mix, seq, rows, width), BF16),
                pltpu.VMEM((mix, seq, rows, width), BF16),
                pltpu.VMEM((mix, seq, rows, width), BF16),
                pltpu.VMEM((mix, seq, rows, width), BF16),
                dma((4, mix - 1)),
                dma((4, mix - 1)),
                dma,
                dma,
                dma,
                dma,
                dma,
                dma((mix,)),
                dma((mix,)),
                dma((mix,)),
                dma((mix,)),
            ],
            compiler_params=pltpu.CompilerParams(
                collective_id=0, has_side_effects=True, vmem_limit_bytes=56 * 1024 * 1024
            ),
        )(tokens, log_forget_rate, w_x, w_z, w_bc, params, conv_bc, w_out)

    return jax.shard_map(
        body,
        mesh=mesh,
        in_specs=(
            P("mix", "seq", None),
            P("mix", "seq", None),
            P(None, "mix"),
            P(None, "mix"),
            P(),
            P(None, "mix"),
            P(),
            P("mix"),
            P("mix"),
            P("mix", None),
        ),
        out_specs=P("mix", "seq", None),
        check_vma=False,
    )
```

time: 171 us -> 38.7 us (0.23)
  waiting for transfers between devices: 47.3 us -> 0 us
  blocking collectives: 38.2 us -> 0 us
  Pallas kernels: 0 us -> 32.4 us
  local copies, waits for them, and re-layouts: 25.3 us -> 4.18 us
  matrix products: 18.3 us -> 0 us
  other arithmetic: 17.5 us -> 1.35 us
  between operations: 14 us -> 0.01 us
  starting transfers between devices: 8.44 us -> 0 us
    all_gather x4 -> x0, waiting for transfers between devices: 46 us -> none  [the longest x1 43.5 us: carried_in(): pieces = jax.tree.map(lambda part: lax.all_gather(part, axis), value)]
    pallas_call x0 -> x1, Pallas kernels: none -> 32.4 us  [body(): pl.pallas_call(functools.partial(kernel, seq, mix), out_shape=jax.ShapeDt...]
    all_gather x3 -> x0, blocking collectives: 31.1 us -> none  [the longest x1 20.7 us: carried_in(): pieces = jax.tree.map(lambda part: lax.all_gather(part, axis), value)]
    dot_general x13 -> x0, matrix products: 18.3 us -> none  [the longest x2 3.95 us: mixture_pass(): jnp.einsum('bqn,bhpn->bqhp', readout_projection_rows.astype(jnp.float32),...]
    select_n x7 -> x0, other arithmetic: 8.38 us -> none  [hop(): jnp.where(position < mine, new, old)]
    ppermute x2 -> x0, starting transfers between devices: 8.32 us -> none  [shifted(): lax.ppermute(value, axis, [(source, source + steps) for source in range(l...]
    unnamed x1 -> x0, blocking collectives: 7.08 us -> none
    reshape x10 -> x0, local copies, waits for them, and re-layouts: 6.36 us -> none  [the longest x4 3.04 us: mixture_pass(): xb = x_act.reshape(count, BLOCK, heads, HEAD_DIM)]
  transfers between devices with their start and end apart: 6 -> 0, of which waited for: 2 -> 0; matrix products, arithmetic and copies ran while one was open for 33% -> 0% of each run, Pallas kernels for 0% -> 0%
where the time goes in v1:
time: 38.7 us; the launch traced here: 37.9 us
  Pallas kernels  32.4 us (84%)
  local copies, waits for them, and re-layouts  4.18 us (11%)
  other arithmetic  1.35 us (3%)
    pallas_call x1, Pallas kernels, body(): pl.pallas_call(functools.partial(kernel, seq, mix), out_shape=jax.ShapeDt...  32.4 us
    unnamed x4, local copies, waits for them, and re-layouts  2.63 us
    concatenate x1, other arithmetic, body(): jnp.concatenate([conv_x, gain[None], jnp.repeat(skip, HEAD_DIM)[None], jn...  1.35 us

profile of v1, /device:TPU:0, one launch (start us, length us, event | category | flops | bytes accessed | tf_op | source)
XLA Modules:
  0.0 37.9 jit_solution(17124983131023364422)
XLA Ops:
  0.0 0.0 copy-start
  0.0 0.1 pad.3.clone
  0.1 0.7 %broadcast_in_dim.10 = bf16[4,64]{1,0:T(4,128)(2,1)S(1)} broadcast(bf16[4]{0:T(256)(128)(2,1)} %param.17), dimensions={0} | broadcast | bytes 520 | tf_op jit(solution)/shard_map/broadcast_in_dim | solution.py:357
  0.8 0.1 broadcast_in_dim_reshape.3
  0.9 0.7 %broadcast_in_dim.9 = bf16[1,256]{1,0:T(2,128)(2,1)S(1)} reshape(bf16[256]{0:T(256)(128)(2,1)} %param.18) | data formatting | bytes 1024 | tf_op jit(solution)/shard_map/broadcast_in_dim | solution.py:356
  1.6 1.3 %maximum_maximum_fusion.par = bf16[16,256]{1,0:T(8,128)(2,1)} fusion(bf16[1,256]{1,0:T(2,128)(2,1)S(1)} %broadcast_in_dim_reshape.3, bf16[1,256]{1,0:T(2,128)(2,1)S(1)} %broadcast_in_dim.9, bf16[4,256]{1,0:T(4,128)(2,1)} %param.15, bf16[16]{0:T(256)(128)(2,1)S(1)} %pad.3.clone), kind=kLoop, calls=%fused_computation | loop fusion | flops 32768 | bytes 11296 | tf_op jit(solution)/shard_map/concatenate | solution.py:353
  2.9 0.0 copy-done
  2.9 0.8 %copy.11.rate = bf16[2,256,16]{2,1,0:T(8,128)(2,1)} copy(bf16[2,256,16]{1,2,0:T(8,128)(2,1)S(1)} %copy-done) | data formatting | bytes 32768 | tf_op args[1]
  3.7 32.4 %shard_map.100 = bf16[2,256,512]{2,1,0:T(8,128)(2,1)} custom-call(bf16[2,256,512]{2,1,0:T(8,128)(2,1)} %tok.1, bf16[2,256,16]{2,1,0:T(8,128)(2,1)} %copy.11.rate, bf16[512,256]{1,0:T(8,128)(2,1)} %wx.1, bf16[512,256]{1,0:T(8,128)(2,1)} %wz.1, bf16[512,128]{1,0:T(8,128)(2,1)} %wbc.1, bf16[16,256]{1,0:T(8,128)(2,1)} %maximum_maximum_fusion.par, ...), custom_call_target="tpu_custom_call" | custom-call | tf_op jit(solution)/shard_map/pallas_call | solution.py:365
  36.1 1.9 %copy.13 = bf16[2,256,512]{2,1,0:T(8,128)(2,1)} copy(bf16[2,256,512]{2,1,0:T(8,128)(2,1)} %shard_map.100) | data formatting | bytes 1048576
  (1 shorter events, 0.0 us)
Async XLA Ops:
  0.0 2.9 %copy-start = (bf16[2,256,16]{1,2,0:T(8,128)(2,1)S(1)}, bf16[2,256,16]{1,2,0:T(8,128)(2,1)}, u32[]{:S(2)}) copy-start(bf16[2,256,16]{1,2,0:T(8,128)(2,1)} %param.11) | copy-start | bytes 49156

commit v2 on v1

--- a/solution.py
+++ b/solution.py
@@ -53,20 +53,27 @@
 
 def kernel(
     seq, mix,
-    tok, rate, wx, wz, wbc, par, cbc, wo, out,
-    halo, wxb, wzb, wob, parb, logs, logsrc, pre, xact, bcs, bts, cums, tails, ecs, rows_t,
+    tok_in, rate, wx_in, wz_in, wbc, cx, cbc, skip, gain, wo_in, out,
+    tok, wx, wz, wo, par, halo, wxb, wzb, wob, parb, logs, logsrc, pre, xact, bcs, bts, cums, tails, ecs, rows_t,
     cbm, first, yloc, sgate, normed, sbuf, rbuf, cbuf, gbuf,
-    bsend, brecv, fsend, hsend, hrecv, lsend, lrecv, asend, arecv, csend, crecv,
+    loads, bsend, brecv, xsend, xrecv, ysend, yrecv, fsend, hsend, hrecv, lsend, lrecv, asend, arecv, csend, crecv,
 ):
     me_s, me_m = lax.axis_index("seq"), lax.axis_index("mix")
     mixtures, length = tok.shape[0], tok.shape[1]
-    width = wx.shape[1]
+    width = wx.shape[2]
     per = width // HEAD_DIM
-    heads = rate.shape[2]
+    heads = rate.shape[1]
     blocks = length // BLOCK
     nrows = STATE // seq
     bits = [1 << i for i in range(mix.bit_length() - 1)]
 
+    local = [
+        pltpu.make_async_copy(src, dst, loads.at[i])
+        for i, (src, dst) in enumerate(((wx_in, wx), (tok_in, tok), (wz_in, wz), (wo_in, wo)))
+    ]
+    for copy in local:
+        copy.start()
+
     barrier = pltpu.get_barrier_semaphore()
     for bit in bits:
         pl.semaphore_signal(barrier, inc=1, device_id={"mix": flipped(me_m, bit)}, device_id_type=MESH)
@@ -75,6 +82,16 @@
     def _(i):
         pl.semaphore_signal(barrier, inc=1, device_id={"seq": (me_s + i) % seq}, device_id_type=MESH)
 
+    lane_head = iota((8, width), 1) // HEAD_DIM
+    skip_row = jnp.zeros((8, width), F32)
+    skip_in = jnp.broadcast_to(skip[...].astype(F32)[None, :], (8, per))
+    for i in range(per):
+        skip_row = jnp.where(lane_head == i, skip_in[:, i : i + 1], skip_row)
+    gain_in = jnp.broadcast_to(gain[...].astype(F32)[None, :], (8, width))
+    place = iota((16 - CONV * 2, width), 0)
+    par[pl.ds(0, CONV), :] = cx[...]
+    par[pl.ds(CONV * 2, 16 - CONV * 2), :] = jnp.where(place == 0, gain_in, skip_row).astype(BF16)
+    par[pl.ds(CONV, CONV), :] = jnp.zeros((CONV, width), BF16)
     pl.semaphore_wait(barrier, len(bits) + seq - 1)
 
     shards = ((wx, wxb), (par, parb), (wz, wzb), (wo, wob))
@@ -94,8 +111,37 @@
     def low_bit(offset):
         return offset & -offset
 
+    top = bits[-1]
+    half, other = me_s % 2, 1 - me_s % 2
+
+    def cross(which):
+        own, slots = shards[which]
+        return pltpu.make_async_remote_copy(
+            src_ref=own.at[half], dst_ref=slots.at[top - 1, half],
+            send_sem=xsend.at[which - 2], recv_sem=xrecv.at[which - 2],
+            device_id={"mix": flipped(me_m, top)}, device_id_type=MESH,
+        )
+
+    def beside(which, part):
+        slots = shards[which][1]
+        return pltpu.make_async_remote_copy(
+            src_ref=slots.at[top - 1, part], dst_ref=slots.at[top - 1, part],
+            send_sem=ysend.at[which - 2], recv_sem=yrecv.at[which - 2],
+            device_id={"seq": flipped(me_s, 1)}, device_id_type=MESH,
+        )
+
+    def is_split(which, offset):
+        return which >= 2 and offset == top
+
+    def crossed(which):
+        cross(which).wait_recv()
+        beside(which, half).start()
+
     def arrived(which, offset):
-        share(which, offset - low_bit(offset), low_bit(offset)).wait_recv()
+        if is_split(which, offset):
+            beside(which, other).wait_recv()
+        else:
+            share(which, offset - low_bit(offset), low_bit(offset)).wait_recv()
         for bit in bits:
             if bit < low_bit(offset):
                 share(which, offset, bit).start()
@@ -105,14 +151,29 @@
         send_sem=hsend, recv_sem=hrecv,
         device_id={"seq": (me_s + 1) % seq}, device_id_type=MESH,
     )
-    rim_copy.start()
-    for which in (1, 0, 2, 3):
+    local[0].wait()
+    for which in (0, 1):
         for bit in reversed(bits):
             share(which, 0, bit).start()
-
-    here = iota((heads, LANES), 0)
-    there = iota((heads, LANES), 1)
-    order = jnp.zeros((heads, LANES), jnp.bool_)
+    local[1].wait()
+
+    @pl.when(me_s < seq - 1)
+    def _():
+        rim_copy.start()
+
+    @pl.when(me_s == 0)
+    def _():
+        halo[...] = jnp.zeros_like(halo)
+
+    for which in (2, 3):
+        local[which].wait()
+        cross(which).start()
+        for bit in bits[:-1]:
+            share(which, 0, bit).start()
+
+    here = iota((LANES, heads), 1)
+    there = iota((LANES, heads), 0)
+    order = jnp.zeros((LANES, heads), jnp.bool_)
     for offset in range(mix):
         actual = me_m
         for bit in bits:
@@ -121,21 +182,25 @@
         order = order | ((there // per == offset) & (here == actual * per + there % per))
     order = order.astype(F32).astype(BF16)
     lower = (iota((BLOCK, BLOCK), 0) >= iota((BLOCK, BLOCK), 1)).astype(F32)
-    lower_b = lower.astype(BF16)
+    upper_b = jnp.transpose(lower).astype(BF16)
 
     totals = []
     for m in range(mixtures):
         device_total = jnp.zeros((1, LANES), F32)
         for b in range(blocks):
             at = pl.ds(b * BLOCK, BLOCK)
-            mine = dot(rate[m, at, :], order)
-            cum = dot(lower_b, mine.astype(BF16))
+            mine = dot(order, rate[m, :, b * BLOCK : (b + 1) * BLOCK])[: heads]
+            cum = dot(mine.astype(BF16), upper_b)
+            gain_log = jnp.log(jnp.sqrt(one_minus_exp(2.0 * mine)))
             gain_in = jnp.sqrt(one_minus_exp(2.0 * mine))
-            last = cum[BLOCK - 1 : BLOCK]
-            cums[m, at, :] = cum
-            ecs[m, at, :] = jnp.exp(cum)
-            tails[m, at, :] = jnp.exp(last - cum) * gain_in
-            rows_t[m * blocks + b] = jnp.transpose(cum - jnp.log(gain_in))
+            tail = jnp.exp(cum[:, BLOCK - 1 :] - cum) * gain_in
+            rows_t[m * blocks + b, pl.ds(0, heads), :] = cum - gain_log
+            blank = jnp.zeros((LANES - heads, BLOCK), F32)
+            cum_t = jnp.transpose(jnp.concatenate([cum, blank], axis=0))
+            cums[m, at, :] = cum_t
+            ecs[m, at, :] = jnp.exp(cum_t)
+            tails[m, at, :] = jnp.transpose(jnp.concatenate([tail, blank], axis=0))
+            last = cum_t[BLOCK - 1 :]
             device_total = device_total + last
             totals.append(last)
         logsrc[pl.ds(m, 1), :] = device_total
@@ -151,8 +216,6 @@
     @pl.loop(1, seq)
     def _(i):
         log_copy((me_s + i) % seq).start()
-
-    inside = jnp.where(me_s > 0, 1.0, 0.0)
 
     def convolve(weight, taps, m, columns):
         total = jnp.zeros((length, columns), F32)
@@ -164,10 +227,13 @@
 
     def project(weight, m, columns):
         edge = dot(halo[m], weight).astype(BF16).astype(F32)
-        pre[m, pl.ds(0, 8), pl.ds(0, columns)] = edge[RIM - 8 :] * inside
+        pre[m, pl.ds(0, 8), pl.ds(0, columns)] = edge[RIM - 8 :]
         pre[m, pl.ds(8, length), pl.ds(0, columns)] = dot(tok[m], weight).astype(BF16).astype(F32)
 
-    rim_copy.wait_recv()
+    @pl.when(me_s > 0)
+    def _():
+        rim_copy.wait_recv()
+
     for m in range(mixtures):
         project(wbc[...], m, 2 * STATE)
         bc = convolve(None, cbc[...], m, 2 * STATE)
@@ -178,11 +244,14 @@
             scores = dot_nt(part[:, STATE:], part[:, :STATE])
             cbm[m * blocks + b] = scores * lower
 
+    def flat(weight):
+        return weight.reshape(weight.shape[0] * weight.shape[1], weight.shape[2])
+
     def spread(offset):
         return (iota((LANES, width), 0) == offset * per + iota((LANES, width), 1) // HEAD_DIM).astype(F32).astype(BF16)
 
     def states(offset):
-        weight, params, expand = held(0, offset)[...], held(1, offset)[...], spread(offset)
+        weight, params, expand = flat(held(0, offset)[...]), held(1, offset)[...], spread(offset)
         lanes = pl.ds(offset * width, width)
         per_mixture = []
         for m in range(mixtures):
@@ -249,7 +318,7 @@
 
     def intra(offset):
         lanes = pl.ds(offset * width, width)
-        skip_row = held(1, offset)[pl.ds(CONV + 1, 1), :].astype(F32)
+        skip_row = held(1, offset)[pl.ds(CONV * 2 + 1, 1), :].astype(F32)
         for m in range(mixtures):
             for b in range(blocks):
                 at = pl.ds(b * BLOCK, BLOCK)
@@ -269,7 +338,7 @@
 
     def gate(offset):
         lanes = pl.ds(offset * width, width)
-        weight = held(2, offset)[...]
+        weight = flat(held(2, offset)[...])
         for m in range(mixtures):
             sgate[m, :, lanes] = silu(dot(tok[m], weight).astype(BF16).astype(F32))
 
@@ -279,7 +348,7 @@
         lanes = pl.ds(offset * width, width)
         wait_all(gbuf.at[offset], crecv.at[offset])
         expand = spread(offset)
-        gain_row = held(1, offset)[pl.ds(CONV, 1), :].astype(F32)
+        gain_row = held(1, offset)[pl.ds(CONV * 2, 1), :].astype(F32)
         for m in range(mixtures):
             state = jnp.concatenate(
                 [gbuf[offset, k].astype(F32)[m * nrows : (m + 1) * nrows] for k in range(seq)], axis=0
@@ -308,34 +377,65 @@
         if offset:
             arrived(which, offset)
 
-    for offset in range(mix):
+    def logs_arrived():
+        some = logs.at[pl.ds(0, seq - 1)]
+        pltpu.make_async_copy(some, some, lrecv).wait()
+
+    for offset in range(top):
         take(1, offset)
         take(0, offset)
         states(offset)
-        if offset == 0:
-            intra(offset)
-    pltpu.make_async_copy(logs.at[pl.ds(0, seq - 1)], logs.at[pl.ds(0, seq - 1)], lrecv).wait()
-    for offset in range(mix):
-        carries(offset)
+        intra(offset)
+    for offset in range(top):
         take(2, offset)
         gate(offset)
-    for offset in range(1, mix):
+    for offset in range(top, mix):
+        take(1, offset)
+        take(0, offset)
+        states(offset)
+    logs_arrived()
+    for offset in range(top):
+        carries(offset)
+        take(3, offset)
+    crossed(2)
+    for offset in range(top, mix):
         intra(offset)
-        take(3, offset)
-    for offset in range(mix):
+        if offset == top:
+            carries(offset)
+            crossed(3)
+    take(2, top)
+    for offset in range(top + 1, mix):
+        carries(offset)
+    finish(0)
+    gate(top)
+    take(3, top)
+    for offset in range(1, top):
         finish(offset)
+    for offset in range(top + 1, mix):
+        take(2, offset)
+        gate(offset)
+    for offset in range(top, mix):
+        finish(offset)
+        if offset > top:
+            take(3, offset)
     for m in range(mixtures):
-        total = jnp.zeros((length, wo.shape[1]), F32)
+        total = jnp.zeros((length, wo.shape[2]), F32)
         for offset in range(mix):
-            total = total + dot(normed[m, :, pl.ds(offset * width, width)], held(3, offset)[...])
+            total = total + dot(normed[m, :, pl.ds(offset * width, width)], flat(held(3, offset)[...]))
         out[m] = total.astype(BF16)
 
-    rim_copy.wait_send()
+    @pl.when(me_s < seq - 1)
+    def _():
+        rim_copy.wait_send()
+
     for which in range(4):
         for offset in range(mix):
             for bit in bits:
-                if offset == 0 or bit < low_bit(offset):
+                if (offset == 0 or bit < low_bit(offset)) and not is_split(which, offset + bit):
                     share(which, offset, bit).wait_send()
+    for which in (2, 3):
+        cross(which).wait_send()
+        beside(which, half).wait_send()
     wait_all(logs, lsend)
     for offset in range(mix):
         wait_all(sbuf.at[offset], asend.at[offset])
@@ -348,26 +448,25 @@
     def body(tokens, log_forget_rate, w_x, w_z, w_bc, conv_x, conv_bc, skip, gain, w_out):
         mixtures, length, depth = tokens.shape
         width = w_x.shape[1]
+        rate = jnp.transpose(log_forget_rate, (0, 2, 1))
         inner = width * mix
         blocks = length // BLOCK
-        params = jnp.concatenate(
-            [
-                conv_x,
-                gain[None],
-                jnp.repeat(skip, HEAD_DIM)[None],
-                jnp.zeros((16 - CONV - 2, width), BF16),
-            ],
-            axis=0,
-        )
+        w_x, w_z, w_out = (w.reshape(2, w.shape[0] // 2, w.shape[1]) for w in (w_x, w_z, w_out))
         vmem = pl.BlockSpec(memory_space=pltpu.VMEM)
+        hbm = pl.BlockSpec(memory_space=pl.ANY)
         dma = pltpu.SemaphoreType.DMA
         rows = mixtures * (STATE // seq)
         return pl.pallas_call(
             functools.partial(kernel, seq, mix),
-            out_shape=jax.ShapeDtypeStruct((mixtures, length, w_out.shape[1]), BF16),
-            in_specs=[vmem] * 8,
+            out_shape=jax.ShapeDtypeStruct((mixtures, length, w_out.shape[2]), BF16),
+            in_specs=[hbm, vmem, hbm, hbm, vmem, vmem, vmem, vmem, vmem, hbm],
             out_specs=vmem,
             scratch_shapes=[
+                pltpu.VMEM(tokens.shape, BF16),
+                pltpu.VMEM(w_x.shape, BF16),
+                pltpu.VMEM(w_z.shape, BF16),
+                pltpu.VMEM(w_out.shape, BF16),
+                pltpu.VMEM((16, width), BF16),
                 pltpu.VMEM((mixtures, RIM, depth), BF16),
                 pltpu.VMEM((mix - 1,) + w_x.shape, BF16),
                 pltpu.VMEM((mix - 1,) + w_z.shape, BF16),
@@ -392,8 +491,13 @@
                 pltpu.VMEM((mix, seq, rows, width), BF16),
                 pltpu.VMEM((mix, seq, rows, width), BF16),
                 pltpu.VMEM((mix, seq, rows, width), BF16),
+                dma((4,)),
                 dma((4, mix - 1)),
                 dma((4, mix - 1)),
+                dma((2,)),
+                dma((2,)),
+                dma((2,)),
+                dma((2,)),
                 dma,
                 dma,
                 dma,
@@ -405,9 +509,9 @@
                 dma((mix,)),
             ],
             compiler_params=pltpu.CompilerParams(
-                collective_id=0, has_side_effects=True, vmem_limit_bytes=56 * 1024 * 1024
+                collective_id=0, has_side_effects=True, vmem_limit_bytes=40 * 1024 * 1024
             ),
-        )(tokens, log_forget_rate, w_x, w_z, w_bc, params, conv_bc, w_out)
+        )(tokens, rate, w_x, w_z, w_bc, conv_x, conv_bc, skip, gain, w_out)
 
     return jax.shard_map(
         body,

time: 38.7 us -> 39.8 us (1.028)
  local copies, waits for them, and re-layouts: 4.18 us -> 7.02 us
  other arithmetic: 1.35 us -> 0 us
    unnamed x4 -> x21, local copies, waits for them, and re-layouts: 2.63 us -> 7.02 us
    broadcast_in_dim x3 -> x0, local copies, waits for them, and re-layouts: 1.39 us -> none  [the longest x1 0.73 us: body(): jnp.repeat(skip, HEAD_DIM)[None]]
    concatenate x1 -> x0, other arithmetic: 1.35 us -> none  [body(): jnp.concatenate([conv_x, gain[None], jnp.repeat(skip, HEAD_DIM)[None], jn...]
where the time goes in v2:
time: 39.8 us; the launch traced here: 39.4 us
  Pallas kernels  32.4 us (81%)
  local copies, waits for them, and re-layouts  7.02 us (18%)
    pallas_call x1, Pallas kernels, body(): pl.pallas_call(functools.partial(kernel, seq, mix), out_shape=jax.ShapeDt...  32.4 us
    unnamed x21, local copies, waits for them, and re-layouts  7.02 us

profile of v2, /device:TPU:0, one launch (start us, length us, event | category | flops | bytes accessed | tf_op | source)
XLA Modules:
  0.0 39.4 jit_solution(10197908140929148535)
XLA Ops:
  0.0 0.0 copy-start.9
  0.0 0.0 copy-start.6
  0.0 0.0 copy-start.7
  0.0 0.0 copy-start.8
  0.0 0.6 %copy-done.9 = bf16[256]{0:T(256)(128)(2,1)S(1)} copy-done((bf16[256]{0:T(256)(128)(2,1)S(1)}, bf16[256]{0:T(256)(128)(2,1)}, u32[]{:S(2)}) %copy-start.9) | copy-done | bytes 536
  0.7 0.0 copy-done.6
  0.7 0.0 copy-done.7
  0.7 0.0 copy-done.8
  0.7 0.0 copy-start
  0.7 1.0 %copy-done = bf16[2,256,512]{2,1,0:T(8,128)(2,1)S(1)} copy-done((bf16[2,256,512]{2,1,0:T(8,128)(2,1)S(1)}, bf16[2,256,512]{2,1,0:T(8,128)(2,1)}, u32[]{:S(2)}) %copy-start) | copy-done | bytes 524312
  1.8 0.0 copy-start.1
  1.8 0.9 %copy-done.1 = bf16[512,256]{1,0:T(8,128)(2,1)S(1)} copy-done((bf16[512,256]{1,0:T(8,128)(2,1)S(1)}, bf16[512,256]{1,0:T(8,128)(2,1)}, u32[]{:S(2)}) %copy-start.1) | copy-done | bytes 262168
  2.7 0.0 copy-start.2
  2.7 0.9 %copy-done.2 = bf16[512,256]{1,0:T(8,128)(2,1)S(1)} copy-done((bf16[512,256]{1,0:T(8,128)(2,1)S(1)}, bf16[512,256]{1,0:T(8,128)(2,1)}, u32[]{:S(2)}) %copy-start.2) | copy-done | bytes 262168
  3.7 0.0 copy-start.3
  3.7 0.9 %copy-done.3 = bf16[256,512]{1,0:T(8,128)(2,1)S(1)} copy-done((bf16[256,512]{1,0:T(8,128)(2,1)S(1)}, bf16[256,512]{1,0:T(8,128)(2,1)}, u32[]{:S(2)}) %copy-start.3) | copy-done | bytes 262168
  4.6 0.0 copy-start.4
  4.6 0.9 %copy-done.4 = bf16[512,128]{1,0:T(8,128)(2,1)S(1)} copy-done((bf16[512,128]{1,0:T(8,128)(2,1)S(1)}, bf16[512,128]{1,0:T(8,128)(2,1)}, u32[]{:S(2)}) %copy-start.4) | copy-done | bytes 131096
  5.5 0.0 copy-start.5
  5.5 0.7 %copy-done.5 = bf16[2,256,16]{1,2,0:T(8,128)(2,1)S(1)} copy-done((bf16[2,256,16]{1,2,0:T(8,128)(2,1)S(1)}, bf16[2,256,16]{1,2,0:T(8,128)(2,1)}, u32[]{:S(2)}) %copy-start.5) | copy-done | bytes 16408
  6.2 32.4 %shard_map.100 = bf16[2,256,512]{2,1,0:T(8,128)(2,1)S(1)} custom-call(bf16[2,256,512]{2,1,0:T(8,128)(2,1)S(1)} %copy-done, bf16[2,16,256]{2,1,0:T(8,128)(2,1)S(1)} %bitcast.7, bf16[2,256,256]{2,1,0:T(8,128)(2,1)S(1)} %bitcast.4, bf16[2,256,256]{2,1,0:T(8,128)(2,1)S(1)} %bitcast.5, bf16[512,128]{1,0:T(8,128)(2,1)S(1)} %copy-done.4, ...), custom_call_target="tpu_custom_call" | custom-call | tf_op jit(solution)/shard_map/pallas_call | solution.py:459
  38.6 0.8 %copy.12 = bf16[2,256,512]{2,1,0:T(8,128)(2,1)} copy(bf16[2,256,512]{2,1,0:T(8,128)(2,1)S(1)} %shard_map.100) | data formatting | bytes 1048576
Async XLA Ops:
  0.0 0.7 %copy-start.9 = (bf16[256]{0:T(256)(128)(2,1)S(1)}, bf16[256]{0:T(256)(128)(2,1)}, u32[]{:S(2)}) copy-start(bf16[256]{0:T(256)(128)(2,1)} %gain.1) | copy-start | bytes 1540
  0.0 0.7 %copy-start.6 = (bf16[4,256]{1,0:T(4,128)(2,1)S(1)}, bf16[4,256]{1,0:T(4,128)(2,1)}, u32[]{:S(2)}) copy-start(bf16[4,256]{1,0:T(4,128)(2,1)} %cx.1) | copy-start | bytes 6148
  0.0 0.7 %copy-start.7 = (bf16[4,128]{1,0:T(4,128)(2,1)S(1)}, bf16[4,128]{1,0:T(4,128)(2,1)}, u32[]{:S(2)}) copy-start(bf16[4,128]{1,0:T(4,128)(2,1)} %cbc.1) | copy-start | bytes 3076
  0.0 0.7 %copy-start.8 = (bf16[4]{0:T(256)(128)(2,1)S(1)}, bf16[4]{0:T(256)(128)(2,1)}, u32[]{:S(2)}) copy-start(bf16[4]{0:T(256)(128)(2,1)} %skip.1) | copy-start | bytes 28
  0.7 1.0 %copy-start = (bf16[2,256,512]{2,1,0:T(8,128)(2,1)S(1)}, bf16[2,256,512]{2,1,0:T(8,128)(2,1)}, u32[]{:S(2)}) copy-start(bf16[2,256,512]{2,1,0:T(8,128)(2,1)} %tok_in.1) | copy-start | bytes 1572868
  1.8 0.9 %copy-start.1 = (bf16[512,256]{1,0:T(8,128)(2,1)S(1)}, bf16[512,256]{1,0:T(8,128)(2,1)}, u32[]{:S(2)}) copy-start(bf16[512,256]{1,0:T(8,128)(2,1)} %param.12) | copy-start | bytes 786436
  2.7 0.9 %copy-start.2 = (bf16[512,256]{1,0:T(8,128)(2,1)S(1)}, bf16[512,256]{1,0:T(8,128)(2,1)}, u32[]{:S(2)}) copy-start(bf16[512,256]{1,0:T(8,128)(2,1)} %param.13) | copy-start | bytes 786436
  3.7 0.9 %copy-start.3 = (bf16[256,512]{1,0:T(8,128)(2,1)S(1)}, bf16[256,512]{1,0:T(8,128)(2,1)}, u32[]{:S(2)}) copy-start(bf16[256,512]{1,0:T(8,128)(2,1)} %param.19) | copy-start | bytes 786436
  4.6 0.9 %copy-start.4 = (bf16[512,128]{1,0:T(8,128)(2,1)S(1)}, bf16[512,128]{1,0:T(8,128)(2,1)}, u32[]{:S(2)}) copy-start(bf16[512,128]{1,0:T(8,128)(2,1)} %wbc.1) | copy-start | bytes 393220
  5.5 0.7 %copy-start.5 = (bf16[2,256,16]{1,2,0:T(8,128)(2,1)S(1)}, bf16[2,256,16]{1,2,0:T(8,128)(2,1)}, u32[]{:S(2)}) copy-start(bf16[2,256,16]{1,2,0:T(8,128)(2,1)} %param.11) | copy-start | bytes 49156

commit v3 on v2

--- a/solution.py
+++ b/solution.py
@@ -53,8 +53,8 @@
 
 def kernel(
     seq, mix,
-    tok_in, rate, wx_in, wz_in, wbc, cx, cbc, skip, gain, wo_in, out,
-    tok, wx, wz, wo, par, halo, wxb, wzb, wob, parb, logs, logsrc, pre, xact, bcs, bts, cums, tails, ecs, rows_t,
+    tok_in, rate_in, wx_in, wz_in, wbc_in, cx_in, cbc_in, skip_in, gain_in, wo_in, out,
+    tok, rate, wx, wz, wbc, cx, cbc, skip, gain, wo, par, halo, wxb, wzb, wob, parb, logs, logsrc, pre, xact, bcs, bts, cums, tails, ecs, rows_t,
     cbm, first, yloc, sgate, normed, sbuf, rbuf, cbuf, gbuf,
     loads, bsend, brecv, xsend, xrecv, ysend, yrecv, fsend, hsend, hrecv, lsend, lrecv, asend, arecv, csend, crecv,
 ):
@@ -69,7 +69,12 @@
 
     local = [
         pltpu.make_async_copy(src, dst, loads.at[i])
-        for i, (src, dst) in enumerate(((wx_in, wx), (tok_in, tok), (wz_in, wz), (wo_in, wo)))
+        for i, (src, dst) in enumerate(
+            (
+                (wx_in, wx), (tok_in, tok), (wz_in, wz), (wo_in, wo), (cx_in, cx),
+                (skip_in, skip), (gain_in, gain), (rate_in, rate), (wbc_in, wbc), (cbc_in, cbc),
+            )
+        )
     ]
     for copy in local:
         copy.start()
@@ -82,15 +87,17 @@
     def _(i):
         pl.semaphore_signal(barrier, inc=1, device_id={"seq": (me_s + i) % seq}, device_id_type=MESH)
 
+    for copy in local[4:7]:
+        copy.wait()
     lane_head = iota((8, width), 1) // HEAD_DIM
     skip_row = jnp.zeros((8, width), F32)
-    skip_in = jnp.broadcast_to(skip[...].astype(F32)[None, :], (8, per))
+    skips = jnp.broadcast_to(skip[...].astype(F32)[None, :], (8, per))
     for i in range(per):
-        skip_row = jnp.where(lane_head == i, skip_in[:, i : i + 1], skip_row)
-    gain_in = jnp.broadcast_to(gain[...].astype(F32)[None, :], (8, width))
+        skip_row = jnp.where(lane_head == i, skips[:, i : i + 1], skip_row)
+    gains = jnp.broadcast_to(gain[...].astype(F32)[None, :], (8, width))
     place = iota((16 - CONV * 2, width), 0)
     par[pl.ds(0, CONV), :] = cx[...]
-    par[pl.ds(CONV * 2, 16 - CONV * 2), :] = jnp.where(place == 0, gain_in, skip_row).astype(BF16)
+    par[pl.ds(CONV * 2, 16 - CONV * 2), :] = jnp.where(place == 0, gains, skip_row).astype(BF16)
     par[pl.ds(CONV, CONV), :] = jnp.zeros((CONV, width), BF16)
     pl.semaphore_wait(barrier, len(bits) + seq - 1)
 
@@ -170,6 +177,9 @@
         cross(which).start()
         for bit in bits[:-1]:
             share(which, 0, bit).start()
+
+    for copy in local[7:]:
+        copy.wait()
 
     here = iota((LANES, heads), 1)
     there = iota((LANES, heads), 0)
@@ -453,19 +463,19 @@
         blocks = length // BLOCK
         w_x, w_z, w_out = (w.reshape(2, w.shape[0] // 2, w.shape[1]) for w in (w_x, w_z, w_out))
         vmem = pl.BlockSpec(memory_space=pltpu.VMEM)
-        hbm = pl.BlockSpec(memory_space=pl.ANY)
+        hbm = pl.BlockSpec(memory_space=pltpu.HBM)
         dma = pltpu.SemaphoreType.DMA
         rows = mixtures * (STATE // seq)
         return pl.pallas_call(
             functools.partial(kernel, seq, mix),
             out_shape=jax.ShapeDtypeStruct((mixtures, length, w_out.shape[2]), BF16),
-            in_specs=[hbm, vmem, hbm, hbm, vmem, vmem, vmem, vmem, vmem, hbm],
+            in_specs=[hbm] * 10,
             out_specs=vmem,
             scratch_shapes=[
-                pltpu.VMEM(tokens.shape, BF16),
-                pltpu.VMEM(w_x.shape, BF16),
-                pltpu.VMEM(w_z.shape, BF16),
-                pltpu.VMEM(w_out.shape, BF16),
+                *[
+                    pltpu.VMEM(a.shape, BF16)
+                    for a in (tokens, rate, w_x, w_z, w_bc, conv_x, conv_bc, skip, gain, w_out)
+                ],
                 pltpu.VMEM((16, width), BF16),
                 pltpu.VMEM((mixtures, RIM, depth), BF16),
                 pltpu.VMEM((mix - 1,) + w_x.shape, BF16),
@@ -491,7 +501,7 @@
                 pltpu.VMEM((mix, seq, rows, width), BF16),
                 pltpu.VMEM((mix, seq, rows, width), BF16),
                 pltpu.VMEM((mix, seq, rows, width), BF16),
-                dma((4,)),
+                dma((10,)),
                 dma((4, mix - 1)),
                 dma((4, mix - 1)),
                 dma((2,)),
@@ -509,7 +519,7 @@
                 dma((mix,)),
             ],
             compiler_params=pltpu.CompilerParams(
-                collective_id=0, has_side_effects=True, vmem_limit_bytes=40 * 1024 * 1024
+                collective_id=0, has_side_effects=True, vmem_limit_bytes=54 * 1024 * 1024
             ),
         )(tokens, rate, w_x, w_z, w_bc, conv_x, conv_bc, skip, gain, w_out)
 

time: 39.8 us -> 35.3 us (0.89)
  local copies, waits for them, and re-layouts: 7.02 us -> 1.87 us
  Pallas kernels: 32.4 us -> 33.2 us
    unnamed x21 -> x1, local copies, waits for them, and re-layouts: 7.02 us -> 1.87 us
    pallas_call x1, Pallas kernels: 32.4 us -> 33.2 us  [body(): pl.pallas_call(functools.partial(kernel, seq, mix), out_shape=jax.ShapeDt...]
where the time goes in v3:
time: 35.3 us; the launch traced here: 35.1 us
  Pallas kernels  33.2 us (94%)
  local copies, waits for them, and re-layouts  1.87 us (5%)
    pallas_call x1, Pallas kernels, body(): pl.pallas_call(functools.partial(kernel, seq, mix), out_shape=jax.ShapeDt...  33.2 us
    unnamed x1, local copies, waits for them, and re-layouts  1.87 us

profile of v3, /device:TPU:0, one launch (start us, length us, event | category | flops | bytes accessed | tf_op | source)
XLA Modules:
  0.0 35.1 jit_solution(13222233694481301947)
XLA Ops:
  0.0 33.2 %shard_map.100 = bf16[2,256,512]{2,1,0:T(8,128)(2,1)} custom-call(bf16[2,256,512]{2,1,0:T(8,128)(2,1)} %tok_in.1, bf16[2,16,256]{2,1,0:T(8,128)(2,1)} %bitcast.7, bf16[2,256,256]{2,1,0:T(8,128)(2,1)} %bitcast.4, bf16[2,256,256]{2,1,0:T(8,128)(2,1)} %bitcast.5, bf16[512,128]{1,0:T(8,128)(2,1)} %wbc_in.1, bf16[4,256]{1,0:T(4,128)(2,1)} %cx_in.1, ...), custom_call_target="tpu_custom_call" | custom-call | tf_op jit(solution)/shard_map/pallas_call | solution.py:469
  33.2 1.9 %copy.12 = bf16[2,256,512]{2,1,0:T(8,128)(2,1)} copy(bf16[2,256,512]{2,1,0:T(8,128)(2,1)} %shard_map.100) | data formatting | bytes 1048576
